TPU v7x, 32 devices: a whole 2x2x4 slice. The times are simulated.
32 devices in a mesh: dp: 4 (over x, core), row: 4 (over z), col: 2 (over y).
Axes of the slice: x: 2, y: 2, z: 4, core: 2. Of those that a mesh axis runs over, the one named last changes fastest.
Arguments:
- states: bfloat16 [8192, 2048], P(('dp', 'row'), 'col'), may hold values from -6 to 6
- keep: int32 [8192], P(('dp', 'row')), may hold values 0 or 1
- cont_ids: int32 [4, 1024], P('dp'), may hold values from 0 to 3, never falling along the last dimension, each value on 1 to 512 neighbouring positions
- answer_len: int32 [4, 4], P('dp'), may hold values from 1 to 512
- teacher: bfloat16 [8192, 2048], P(('dp', 'row'), 'col'), may hold values from -6 to 6
- out_grad: bfloat16 [8192, 2048], P(('dp', 'row'), 'col'), may hold values from -6 to 6
- gain_attn: float32 [2048], P('col'), may hold values from 0.5 to 1.5
- w_query: bfloat16 [2048, 2048], P('col', 'row'), may hold values from -0.125 to 0.125
- key_projection: bfloat16 [2048, 512], P('col', 'row'), may hold values from -0.125 to 0.125
- value_projection: bfloat16 [2048, 512], P('col', 'row'), may hold values from -0.125 to 0.125
- w_out: bfloat16 [2048, 2048], P('row', 'col'), may hold values from -1.5 to 1.5
- gain_ffn: float32 [2048], P('col'), may hold values from 0.5 to 1.5
- w_gate: bfloat16 [2048, 5632], P('col', 'row'), may hold values from -0.125 to 0.125
- w_up: bfloat16 [2048, 5632], P('col', 'row'), may hold values from -0.125 to 0.125
- w_down: bfloat16 [5632, 2048], P('row', 'col'), may hold values from -0.078125 to 0.078125
Outputs:
- output: bfloat16 [8192, 2048], P(('dp', 'row'), 'col')
- loss: float32 [], replicated
- grad_states: float32 [8192, 2048], P(('dp', 'row'), 'col')
- grad_gain_attn: float32 [2048], P('col')
- grad_query: float32 [2048, 2048], P('col', 'row')
- grad_key: float32 [2048, 512], P('col', 'row')
- grad_value: float32 [2048, 512], P('col', 'row')
- grad_out: float32 [2048, 2048], P('row', 'col')
- grad_gain_ffn: float32 [2048], P('col')
- grad_gate: float32 [2048, 5632], P('col', 'row')
- grad_up: float32 [2048, 5632], P('col', 'row')
- grad_down: float32 [5632, 2048], P('row', 'col')
Inputs may be any that keep to these rules, and one draw needn't show every extreme that they name: `cont_ids`: in each group the continuation numbers never fall along the tokens, and each continuation has 1 to 512 tokens.
All inputs are finite; a program needn't handle non-finite values. No bound on the sum of `keep` on one device may be relied on, other than what follows from the above.
Results may differ from a plain program's by a relative error of at most 0.019.
Values may be sent and summed in bfloat16 or wider, within the bound.
No kernel may reach another device: no remote copies, remote signals or barrier semaphores. Data moves between devices by JAX's collectives and lax.ppermute only.
A program may use at most 192 MiB of HBM per device.

v0:
```python
import jax
import jax.numpy as jnp
from jax import lax
from jax.sharding import PartitionSpec as P

MODEL_WIDTH = 2048
HEAD_SIZE = 128
PROMPT = 1024
EPSILON = 1e-05
MASKED = -1e30
ROPE_BASE = 10000.0


def rows_of(values, start, count, axis=0):
    return lax.dynamic_slice_in_dim(values, start, count, axis)


def token_layout(cont_ids, answer_len):
    groups, cont_tokens = cont_ids.shape
    labels = jnp.arange(answer_len.shape[1], dtype=jnp.int32)
    starts = jnp.sum((cont_ids[:, None, :] < labels[None, :, None]).astype(jnp.int32), axis=2)
    member = (cont_ids[:, :, None] == labels[None, None, :]).astype(jnp.int32)
    own_start = jnp.sum(member * starts[:, None, :], axis=2)
    own_limit = jnp.sum(member * answer_len[:, None, :], axis=2)
    offset = jnp.arange(cont_tokens, dtype=jnp.int32)[None, :] - own_start
    prompt_pos = jnp.arange(PROMPT, dtype=jnp.int32)[None, :]
    positions = jnp.concatenate([prompt_pos, PROMPT + offset], axis=1).reshape(-1)
    segment = jnp.concatenate(
        [jnp.full((groups, PROMPT), -1, dtype=jnp.int32), cont_ids], axis=1
    ).reshape(-1)
    counted = jnp.concatenate(
        [jnp.ones((groups, PROMPT), jnp.int32), (offset < own_limit).astype(jnp.int32)], axis=1
    ).reshape(-1)
    return (positions, segment, counted)


def rotary(values, positions, sign):
    half = values.shape[-1] // 2
    freqs = ROPE_BASE ** (-2.0 * jnp.arange(half, dtype=jnp.float32) / values.shape[-1])
    angles = positions.astype(jnp.float32)[:, None] * freqs[None, :]
    cosine = jnp.cos(angles)[:, None, :]
    sine = sign * jnp.sin(angles)[:, None, :]
    first = values[..., :half]
    second = values[..., half:]
    return jnp.concatenate(
        [first * cosine - second * sine, second * cosine + first * sine], axis=-1
    )


def visible(query_index, query_segment, key_index, key_segment):
    earlier = key_index[None, :] <= query_index[:, None]
    shared = (key_segment[None, :] < 0) | (key_segment[None, :] == query_segment[:, None])
    return earlier & shared


def feature_sum(values):
    return lax.psum(values, "col")


def gather_rows(values):
    return lax.all_gather(values, "row", axis=0, tiled=True)


def gather_cols(values):
    return lax.all_gather(values, "col", axis=0, tiled=True)


def partial_cols(term, count):
    return lax.psum_scatter(
        term(jnp.int32(0), count * lax.axis_size("col")), "col", scatter_dimension=0, tiled=True
    )


def partial_rows(term, count):
    return lax.psum_scatter(
        term(jnp.int32(0), count * lax.axis_size("row")), "row", scatter_dimension=0, tiled=True
    )


def body(
    states,
    keep,
    cont_ids,
    answer_len,
    teacher,
    out_grad,
    gain_attn,
    w_query,
    key_projection,
    value_projection,
    w_out,
    gain_ffn,
    w_gate,
    w_up,
    w_down,
):
    local_rows = states.shape[0]
    whole_rows = local_rows * lax.axis_size("row")
    query_rows = whole_rows // lax.axis_size("col")
    group_tokens = PROMPT + cont_ids.shape[1]
    key_heads = key_projection.shape[1] // HEAD_SIZE
    heads_per_group = w_query.shape[1] // key_projection.shape[1]
    query_width = w_query.shape[1]
    scale = HEAD_SIZE ** (-0.5)
    block = min(512, query_rows)
    blocks = query_rows // block
    positions, segment, counted = token_layout(cont_ids, answer_len)
    token_index = jnp.arange(whole_rows, dtype=jnp.int32)
    row_start = lax.axis_index("row") * local_rows
    col_start = lax.axis_index("col") * query_rows
    counted_here = rows_of(counted, row_start, local_rows).astype(jnp.float32)[:, None]
    query_pos = rows_of(positions, col_start, query_rows)
    keep_here = keep.astype(jnp.float32)[:, None]
    states_f = states.astype(jnp.float32)
    scale_attn = lax.rsqrt(
        feature_sum(jnp.sum(states_f * states_f, axis=1)) / MODEL_WIDTH + EPSILON
    )[:, None]
    normed_attn = (states_f * scale_attn * gain_attn[None, :]).astype(jnp.bfloat16)
    normed_all = gather_rows(normed_attn)
    w_kv = jnp.concatenate([key_projection, value_projection], axis=1)
    query_raw = partial_cols(
        lambda start, count: jnp.dot(
            rows_of(normed_all, start, count), w_query, preferred_element_type=jnp.float32
        ),
        query_rows,
    )
    kv_raw = lax.psum(jnp.dot(normed_all, w_kv, preferred_element_type=jnp.float32), "col")
    queries = (
        rotary(
            query_raw.reshape(query_rows, key_heads * heads_per_group, HEAD_SIZE), query_pos, 1.0
        )
        .astype(jnp.bfloat16)
        .reshape(query_rows, key_heads, heads_per_group, HEAD_SIZE)
    )
    keys = rotary(
        kv_raw[:, : key_heads * HEAD_SIZE].reshape(whole_rows, key_heads, HEAD_SIZE), positions, 1.0
    ).astype(jnp.bfloat16)
    values = (
        kv_raw[:, key_heads * HEAD_SIZE :]
        .reshape(whole_rows, key_heads, HEAD_SIZE)
        .astype(jnp.bfloat16)
    )

    def context_of(index):
        first = col_start + index * block
        key_first = first // group_tokens * group_tokens
        query_block = rows_of(queries, index * block, block)
        key_group = rows_of(keys, key_first, group_tokens)
        value_group = rows_of(values, key_first, group_tokens)
        raw = (
            jnp.einsum("qgjd,kgd->gjqk", query_block, key_group, preferred_element_type=jnp.float32)
            * scale
        )
        mask = visible(
            rows_of(token_index, first, block),
            rows_of(segment, first, block),
            rows_of(token_index, key_first, group_tokens),
            rows_of(segment, key_first, group_tokens),
        )
        scores = jnp.where(mask[None, None], raw, MASKED)
        return (query_block, key_group, value_group, scores, key_first)

    def attend(index):
        query_block, key_group, value_group, scores, key_first = context_of(index)
        peak = jnp.max(scores, axis=-1, keepdims=True)
        exponent = jnp.exp(scores - peak)
        totals = jnp.sum(exponent, axis=-1, keepdims=True)
        weights = (exponent / totals).astype(jnp.bfloat16)
        mixed = jnp.einsum(
            "gjqk,kgd->qgjd", weights, value_group, preferred_element_type=jnp.float32
        )
        return (mixed, peak + jnp.log(totals))

    mixed_blocks, log_totals = lax.map(attend, jnp.arange(blocks, dtype=jnp.int32))
    attn_context = mixed_blocks.reshape(query_rows, query_width).astype(jnp.bfloat16)
    context_all = gather_cols(attn_context)
    attention = partial_rows(
        lambda start, count: jnp.dot(
            rows_of(context_all, start, count), w_out, preferred_element_type=jnp.float32
        ),
        local_rows,
    )
    hidden_res = states_f + keep_here * attention
    scale_ffn = lax.rsqrt(
        feature_sum(jnp.sum(hidden_res * hidden_res, axis=1)) / MODEL_WIDTH + EPSILON
    )[:, None]
    normed_ffn = (hidden_res * scale_ffn * gain_ffn[None, :]).astype(jnp.bfloat16)
    ffn_all = gather_rows(normed_ffn)
    w_pair = jnp.concatenate([w_gate, w_up], axis=1)
    inner = w_gate.shape[1]
    gate_up = partial_cols(
        lambda start, count: jnp.dot(
            rows_of(ffn_all, start, count), w_pair, preferred_element_type=jnp.float32
        ),
        query_rows,
    )
    gate = gate_up[:, :inner]
    up_proj = gate_up[:, inner:]
    sigma = jax.nn.sigmoid(gate)
    swish = gate * sigma
    hidden = (swish * up_proj).astype(jnp.bfloat16)
    hidden_all = gather_cols(hidden)
    feed = partial_rows(
        lambda start, count: jnp.dot(
            rows_of(hidden_all, start, count), w_down, preferred_element_type=jnp.float32
        ),
        local_rows,
    )
    result = hidden_res + keep_here * feed
    error = result - teacher.astype(jnp.float32)
    own_count = jnp.where(lax.axis_index("col") == 0, jnp.sum(counted_here), 0.0)
    error_total, token_count_sum = lax.psum(
        (jnp.sum(counted_here * error * error), own_count), ("dp", "row", "col")
    )
    loss = error_total / (token_count_sum * MODEL_WIDTH)
    grad_result = (
        out_grad.astype(jnp.float32) + 2.0 / (token_count_sum * MODEL_WIDTH) * counted_here * error
    )
    grad_feed = (keep_here * grad_result).astype(jnp.bfloat16)
    grad_feed_all = gather_rows(grad_feed)
    grad_down = jnp.einsum(
        "tf,td->fd", hidden_all, grad_feed_all, preferred_element_type=jnp.float32
    )
    grad_hidden = partial_cols(
        lambda start, count: jnp.einsum(
            "td,fd->tf",
            rows_of(grad_feed_all, start, count),
            w_down,
            preferred_element_type=jnp.float32,
        ),
        query_rows,
    )
    grad_gate_in = grad_hidden * up_proj * sigma * (1.0 + gate * (1.0 - sigma))
    grad_up_in = grad_hidden * swish
    grad_pair = jnp.concatenate([grad_gate_in, grad_up_in], axis=1).astype(jnp.bfloat16)
    grad_pair_all = gather_cols(grad_pair)
    grad_w_pair = jnp.einsum(
        "td,tf->df", ffn_all, grad_pair_all, preferred_element_type=jnp.float32
    )
    grad_normed_ffn = partial_rows(
        lambda start, count: jnp.einsum(
            "tf,df->td",
            rows_of(grad_pair_all, start, count),
            w_pair,
            preferred_element_type=jnp.float32,
        ),
        local_rows,
    )
    grad_gain_ffn = jnp.sum(grad_normed_ffn * hidden_res * scale_ffn, axis=0)
    weighted_ffn = grad_normed_ffn * gain_ffn[None, :]
    inner_ffn = feature_sum(jnp.sum(weighted_ffn * hidden_res, axis=1))[:, None]
    grad_hidden_res = (
        grad_result + scale_ffn * weighted_ffn - hidden_res * scale_ffn**3 * inner_ffn / MODEL_WIDTH
    )
    grad_attention = (keep_here * grad_hidden_res).astype(jnp.bfloat16)
    grad_att_all = gather_rows(grad_attention)
    grad_out = jnp.einsum(
        "to,td->od", context_all, grad_att_all, preferred_element_type=jnp.float32
    )
    grad_context = partial_cols(
        lambda start, count: jnp.einsum(
            "td,od->to",
            rows_of(grad_att_all, start, count),
            w_out,
            preferred_element_type=jnp.float32,
        ),
        query_rows,
    )
    grad_context = grad_context.astype(jnp.bfloat16).reshape(
        query_rows, key_heads, heads_per_group, HEAD_SIZE
    )

    def attend_back(carry, item):
        index, log_total = item
        query_block, key_group, value_group, scores, key_first = context_of(index)
        grad_block = rows_of(grad_context, index * block, block)
        probs = jnp.exp(scores - log_total)
        grad_probs = jnp.einsum(
            "qgjd,kgd->gjqk", grad_block, value_group, preferred_element_type=jnp.float32
        )
        row_dot = jnp.sum(probs * grad_probs, axis=-1, keepdims=True)
        grad_scores = (probs * (grad_probs - row_dot)).astype(jnp.bfloat16)
        grad_query_block = (
            jnp.einsum("gjqk,kgd->qgjd", grad_scores, key_group, preferred_element_type=jnp.float32)
            * scale
        )
        grad_key_group = (
            jnp.einsum(
                "gjqk,qgjd->kgd", grad_scores, query_block, preferred_element_type=jnp.float32
            )
            * scale
        )
        grad_value_group = jnp.einsum(
            "gjqk,qgjd->kgd",
            probs.astype(jnp.bfloat16),
            grad_block,
            preferred_element_type=jnp.float32,
        )
        pair = jnp.concatenate([grad_key_group, grad_value_group], axis=1)
        updated = rows_of(carry, key_first, group_tokens) + pair
        return (updated, grad_query_block)

    start_carry = jnp.zeros((whole_rows, 2 * key_heads, HEAD_SIZE), jnp.float32)
    grad_kv_part, grad_query_blocks = lax.scan(
        attend_back, start_carry, (jnp.arange(blocks, dtype=jnp.int32), log_totals)
    )
    grad_kv_sum = (
        lax.psum(
            grad_kv_part.reshape(whole_rows, 2 * key_heads * HEAD_SIZE).astype(jnp.bfloat16), "col"
        )
        .astype(jnp.float32)
        .reshape(whole_rows, 2 * key_heads, HEAD_SIZE)
    )
    grad_keys = rotary(grad_kv_sum[:, :key_heads], positions, -1.0)
    grad_kv = (
        jnp.concatenate([grad_keys, grad_kv_sum[:, key_heads:]], axis=1)
        .reshape(whole_rows, 2 * key_heads * HEAD_SIZE)
        .astype(jnp.bfloat16)
    )
    grad_queries = (
        rotary(
            grad_query_blocks.reshape(query_rows, key_heads * heads_per_group, HEAD_SIZE),
            query_pos,
            -1.0,
        )
        .reshape(query_rows, query_width)
        .astype(jnp.bfloat16)
    )
    grad_queries_all = gather_cols(grad_queries)
    grad_query = jnp.einsum(
        "td,tq->dq", normed_all, grad_queries_all, preferred_element_type=jnp.float32
    )
    grad_kv_weight = jnp.einsum(
        "td,tk->dk", normed_all, grad_kv, preferred_element_type=jnp.float32
    )
    grad_key = grad_kv_weight[:, : key_heads * HEAD_SIZE]
    grad_value = grad_kv_weight[:, key_heads * HEAD_SIZE :]

    def back_terms(start, count):
        from_queries = jnp.einsum(
            "tq,dq->td",
            rows_of(grad_queries_all, start, count),
            w_query,
            preferred_element_type=jnp.float32,
        )
        from_kv = jnp.einsum(
            "tk,dk->td", rows_of(grad_kv, start, count), w_kv, preferred_element_type=jnp.float32
        )
        return from_queries + from_kv

    grad_normed_attn = partial_rows(back_terms, local_rows)
    grad_gain_attn = jnp.sum(grad_normed_attn * states_f * scale_attn, axis=0)
    weighted_attn = grad_normed_attn * gain_attn[None, :]
    inner_attn = feature_sum(jnp.sum(weighted_attn * states_f, axis=1))[:, None]
    grad_states = (
        grad_hidden_res
        + scale_attn * weighted_attn
        - states_f * scale_attn**3 * inner_attn / MODEL_WIDTH
    )
    gain_attn_sum, gain_ffn_sum = lax.psum((grad_gain_attn, grad_gain_ffn), ("dp", "row"))
    summed = (
        lax.psum(grad_query.astype(jnp.bfloat16), "dp").astype(jnp.float32),
        lax.psum(grad_key.astype(jnp.bfloat16), "dp").astype(jnp.float32),
        lax.psum(grad_value.astype(jnp.bfloat16), "dp").astype(jnp.float32),
        lax.psum(grad_out.astype(jnp.bfloat16), "dp").astype(jnp.float32),
        lax.psum(grad_w_pair[:, :inner].astype(jnp.bfloat16), "dp").astype(jnp.float32),
        lax.psum(grad_w_pair[:, inner:].astype(jnp.bfloat16), "dp").astype(jnp.float32),
        lax.psum(grad_down.astype(jnp.bfloat16), "dp").astype(jnp.float32),
    )
    return (
        result.astype(jnp.bfloat16),
        loss,
        grad_states,
        gain_attn_sum,
        summed[0],
        summed[1],
        summed[2],
        summed[3],
        gain_ffn_sum,
        summed[4],
        summed[5],
        summed[6],
    )


def solution(mesh):
    return jax.shard_map(
        body,
        mesh=mesh,
        in_specs=(
            P(("dp", "row"), "col"),
            P(("dp", "row")),
            P("dp", None),
            P("dp", None),
            P(("dp", "row"), "col"),
            P(("dp", "row"), "col"),
            P("col"),
            P("col", "row"),
            P("col", "row"),
            P("col", "row"),
            P("row", "col"),
            P("col"),
            P("col", "row"),
            P("col", "row"),
            P("row", "col"),
        ),
        out_specs=(
            P(("dp", "row"), "col"),
            P(),
            P(("dp", "row"), "col"),
            P("col"),
            P("col", "row"),
            P("col", "row"),
            P("col", "row"),
            P("row", "col"),
            P("col"),
            P("col", "row"),
            P("col", "row"),
            P("row", "col"),
        ),
        check_vma=False,
    )
```

profile of v0, /device:TPU:0, one launch (start us, length us, event | category | flops | bytes accessed | tf_op | source)
XLA Modules:
  0.0 2396.0 jit_solution(15382242776699901373)
XLA Ops:
  8.9 5.9 psum.119
  20.5 80.6 %all-gather.9.cloned.1.call-done = bf16[2048,1024]{1,0:T(8,128)(2,1)} async-done(((bf16[512,1024]{1,0:T(8,128)(2,1)}), bf16[2048,1024]{1,0:T(8,128)(2,1)}) %all-gather.9.cloned.1.call-update) | async-done | bytes 4194320 | tf_op jit(solution)/shard_map/all_gather | solution.py:61
  106.0 6.8 fusion.91
  118.2 49.4 %all-reduce.9.cloned.1.call-done = f32[2048,256]{0,1:T(8,128)} async-done(((f32[2048,256]{0,1:T(8,128)}), f32[2048,256]{0,1:T(8,128)}) %all-reduce.9.cloned.1.call-update) | async-done | bytes 2097168 | tf_op jit(solution)/shard_map/psum | solution.py:127
  177.6 47.3 %reduce-scatter.9.cloned.1.call-done = f32[1024,512]{1,0:T(8,128)} async-done(((f32[2048,512]{1,0:T(8,128)}), f32[1024,512]{1,0:T(8,128)}) %reduce-scatter.9.cloned.1.call-update) | async-done | bytes 2097168 | tf_op jit(solution)/shard_map/reduce_scatter | solution.py:69
  233.5 36.7 %while.27 = (s32[]{:T(128)}, bf16[2,512,1,4,128]{4,1,3,2,0:T(8,128)(2,1)}, f32[2,1,4,512,1]{3,2,4,1,0:T(4,128)S(1)}, s32[2048]{0:T(1024)S(1)}, s32[2]{0:T(128)S(...) while((s32[]{:T(128)}, ...), condition=%wide.region_9.10_spmd.clone, body=%wide.region_6.9_spmd.clone.sunk | while | flops 2202009600 | bytes 65642824 | solution.py:174
  245.3 5.5 fusion.154
  263.7 5.5 fusion.154
  273.8 32.8 %all-gather.11.cloned.1.call-done = bf16[2048,512]{1,0:T(8,128)(2,1)} async-done(((bf16[1024,512]{1,0:T(8,128)(2,1)}), bf16[2048,512]{1,0:T(8,128)(2,1)}) %all-gather.11.cloned.1.call-update) | async-done | bytes 2097168 | tf_op jit(solution)/shard_map/all_gather | solution.py:65
  306.7 7.5 fusion.93
  314.8 144.0 %reduce-scatter.11.cloned.1.call-done = f32[512,1024]{1,0:T(8,128)} async-done(((f32[2048,1024]{1,0:T(8,128)}), f32[512,1024]{1,0:T(8,128)}) %reduce-scatter.11.cloned.1.call-update) | async-done | bytes 2097168 | tf_op jit(solution)/shard_map/reduce_scatter | solution.py:75
  475.8 76.0 %all-gather.13.cloned.1.call-done = bf16[2048,1024]{1,0:T(8,128)(2,1)} async-done(((bf16[512,1024]{1,0:T(8,128)(2,1)}), bf16[2048,1024]{1,0:T(8,128)(2,1)}) %all-gather.13.cloned.1.call-update) | async-done | bytes 4194320 | tf_op jit(solution)/shard_map/all_gather | solution.py:61
  551.8 19.7 fusion.94
  571.6 255.4 %reduce-scatter.13.cloned.1.call-done = f32[1024,2816]{1,0:T(8,128)} async-done(((f32[2048,2816]{1,0:T(8,128)}), f32[1024,2816]{1,0:T(8,128)}) %reduce-scatter.13.cloned.1.call-update) | async-done | bytes 11534352 | tf_op jit(solution)/shard_map/reduce_scatter | solution.py:69
  827.0 6.3 multiply_convert_fusion.2
  833.3 74.6 %all-gather.15.cloned.1.call-done = bf16[2048,1408]{1,0:T(8,128)(2,1)} async-done(((bf16[1024,1408]{1,0:T(8,128)(2,1)}), bf16[2048,1408]{1,0:T(8,128)(2,1)}) %all-gather.15.cloned.1.call-update) | async-done | bytes 5767184 | tf_op jit(solution)/shard_map/all_gather | solution.py:65
  907.9 10.7 fusion.95
  920.6 142.7 %reduce-scatter.15.cloned.1.call-done = f32[512,1024]{1,0:T(8,128)} async-done(((f32[2048,1024]{1,0:T(8,128)}), f32[512,1024]{1,0:T(8,128)}) %reduce-scatter.15.cloned.1.call-update) | async-done | bytes 2097168 | tf_op jit(solution)/shard_map/reduce_scatter | solution.py:75
  1068.3 41.1 %all-reduce.2 = (f32[]{:T(128)}, f32[]{:T(128)}) all-reduce(f32[]{:T(128)} %get-tuple-element.352, f32[]{:T(128)S(6)} %select_n.47), channel_id=1, replica_groups=mesh['dp'=4,'row'=4,'col'=2] {'dp','row','col'}, use_global_device_ids=true, to_apply=%region_17.18 | all-reduce | flops 2 | bytes 16 | tf_op jit(solution)/shard_map/psum | solution.py:212
  1113.8 80.8 %all-gather.17.cloned.1.call-done = bf16[2048,1024]{1,0:T(8,128)(2,1)} async-done(((bf16[512,1024]{1,0:T(8,128)(2,1)}), bf16[2048,1024]{1,0:T(8,128)(2,1)}) %all-gather.17.cloned.1.call-update) | async-done | bytes 4194320 | tf_op jit(solution)/shard_map/all_gather | solution.py:61
  1194.7 11.2 fusion.96
  1205.9 131.8 %reduce-scatter.17.cloned.1.call-done = f32[1024,1408]{1,0:T(8,128)} async-done(((f32[2048,1408]{1,0:T(8,128)}), f32[1024,1408]{1,0:T(8,128)}) %reduce-scatter.17.cloned.1.call-update) | async-done | bytes 5767184 | tf_op jit(solution)/shard_map/reduce_scatter | solution.py:69
  1337.7 7.4 multiply_convert_fusion.1
  1348.1 141.1 %all-gather.19.cloned.1.call-done = bf16[2048,2816]{1,0:T(8,128)(2,1)} async-done(((bf16[1024,2816]{1,0:T(8,128)(2,1)}), bf16[2048,2816]{1,0:T(8,128)(2,1)}) %all-gather.19.cloned.1.call-update) | async-done | bytes 11534352 | tf_op jit(solution)/shard_map/all_gather | solution.py:65
  1489.2 18.0 fusion.97
  1507.3 144.6 %reduce-scatter.19.cloned.1.call-done = f32[512,1024]{1,0:T(8,128)} async-done(((f32[2048,1024]{1,0:T(8,128)}), f32[512,1024]{1,0:T(8,128)}) %reduce-scatter.19.cloned.1.call-update) | async-done | bytes 2097168 | tf_op jit(solution)/shard_map/reduce_scatter | solution.py:75
  1659.5 5.5 multiply_convert_fusion.3
  1665.1 81.6 %all-gather.21.cloned.1.call-done = bf16[2048,1024]{1,0:T(8,128)(2,1)} async-done(((bf16[512,1024]{1,0:T(8,128)(2,1)}), bf16[2048,1024]{1,0:T(8,128)(2,1)}) %all-gather.21.cloned.1.call-update) | async-done | bytes 4194320 | tf_op jit(solution)/shard_map/all_gather | solution.py:61
  1746.7 6.9 fusion.98
  1753.7 10.9 convolution_convert_fusion.1
  1764.5 42.0 %reduce-scatter.21.cloned.1.call-done = f32[1024,512]{1,0:T(8,128)} async-done(((f32[2048,512]{1,0:T(8,128)}), f32[1024,512]{1,0:T(8,128)}) %reduce-scatter.21.cloned.1.call-update) | async-done | bytes 2097168 | tf_op jit(solution)/shard_map/reduce_scatter | solution.py:69
  1809.4 100.4 %while.28 = (s32[]{:T(128)}, f32[2048,2,128]{0,2,1:T(8,128)}, f32[2,512,1,4,128]{4,1,0,3,2:T(8,128)}, s32[2]{0:T(128)S(1)}, bf16[1024,1,4,128]{3,0,2,1:T(8,128)(...) while((s32[]{:T(128)}, f32[2048,2,128]{0,2,1:T(8,128)}, ...), condition=%wide.region_27.28_spmd.clone.clone, body=%wide.region_25.27_spmd.clone.clone.sunk | while | flops 5437915136 | bytes 244941232 | solution.py:304
  1817.1 5.8 copy-done.2
  1822.9 5.1 fusion.163
  1828.0 12.1 fusion.164
  1840.1 12.1 fusion.165
  1867.0 5.8 copy-done.2
  1872.8 5.1 fusion.163
  1877.9 12.1 fusion.164
  1889.9 12.1 fusion.165
  1912.6 19.1 convolution_convert_fusion
  1934.5 5.8 fusion.88
  1943.6 9.2 all-reduce.11.cloned.1.call-done
  1959.2 28.7 %all-gather.23.cloned.1.call-done = bf16[2048,512]{0,1:T(8,128)(2,1)} async-done(((bf16[1024,512]{0,1:T(8,128)(2,1)}), bf16[2048,512]{0,1:T(8,128)(2,1)}) %all-gather.23.cloned.1.call-update) | async-done | bytes 2097168 | tf_op jit(solution)/shard_map/all_gather | solution.py:65
  1987.9 6.2 convolution_convert_fusion.3
  2004.7 191.2 %all-reduce.13.cloned.1.call-done = (bf16[1024,512]{1,0:T(8,128)(2,1)}, bf16[1024,128]{1,0:T(8,128)(2,1)}, bf16[1024,128]{1,0:T(8,128)(2,1)}, bf16[512,1024]{1,0...) async-done(((bf16[1024,512]{1,0:T(8,128)(2,1)}, bf16[1024,128]{1,0:T(8,128)(2,1)}, bf16[1024,128]{1,0:T(8,128)(2,1)}, ...) | async-done | bytes 11272208 | tf_op jit(solution)/shard_map/psum | solution.py:362
  2214.1 128.9 %reduce-scatter.23.cloned.1.call-done = f32[512,1024]{1,0:T(8,128)} async-done(((f32[2048,1024]{1,0:T(8,128)}), f32[512,1024]{1,0:T(8,128)}) %reduce-scatter.23.cloned.1.call-update) | async-done | bytes 2097168 | tf_op jit(solution)/shard_map/reduce_scatter | solution.py:75
  2350.2 33.3 %all-reduce.3 = (f32[1024]{0:T(1024)}, f32[1024]{0:T(1024)}) all-reduce(f32[1024]{0:T(1024)S(1)} %get-tuple-element.289, f32[1024]{0:T(1024)S(1)} %copy-done.33), channel_id=1, replica_groups=mesh['dp'=4,'row'=4,'col'=2] {'dp','row'}, use_global_device_ids=true, to_apply=%region_33.34 | all-reduce | flops 2048 | bytes 16384 | tf_op jit(solution)/shard_map/psum | solution.py:360
  (252 shorter events, 188.9 us)
Async XLA Ops:
  7.2 900.8 %copy-start = (bf16[1408,1024]{1,0:T(8,128)(2,1)S(1)}, bf16[1408,1024]{1,0:T(8,128)(2,1)}, u32[]{:S(2)}) copy-start(bf16[1408,1024]{1,0:T(8,128)(2,1)} %param.33) | copy-start | bytes 8650756
  7.2 94.0 %all-gather.9.cloned.1.call-start = ((), (), s32[]{:S(2)}) async-start(), calls=%async_computation.8 | async-start | bytes 5242880 | tf_op jit(solution)/shard_map/all_gather | solution.py:61
  18.5 149.1 %all-reduce.9.cloned.1.call-start = ((), (), s32[]{:S(2)}) async-start(), calls=%async_computation.10 | async-start | bytes 4194304 | tf_op jit(solution)/shard_map/psum | solution.py:127
  20.5 85.4 %copy-start.19 = (bf16[1024,256]{1,0:T(8,128)(2,1)}, bf16[1024,256]{1,0:T(8,128)(2,1)S(1)}, u32[]{:S(2)}) copy-start(bf16[1024,256]{1,0:T(8,128)(2,1)S(1)} %constant_dynamic-update-slice_fusion) | copy-start | bytes 1572868
  106.0 118.9 %reduce-scatter.9.cloned.1.call-start = ((), (), s32[]{:S(2)}) async-start(), calls=%async_computation.9 | async-start | bytes 6291456 | tf_op jit(solution)/shard_map/reduce_scatter | solution.py:69
  112.9 193.8 %all-gather.11.cloned.1.call-start = ((), (), s32[]{:S(2)}) async-start(), calls=%async_computation.11 | async-start | bytes 3145728 | tf_op jit(solution)/shard_map/all_gather | solution.py:65
  113.6 58.7 %copy-start.36 = (f32[64]{0:T(128)}, f32[64]{0:T(128)S(1)}, u32[]{:S(2)}) copy-start(f32[64]{0:T(128)S(1)} %multiply_power_fusion) | copy-start | bytes 772
  115.0 57.3 %copy-start.24 = (f32[1,2048]{1,0:T(1,128)}, f32[1,2048]{1,0:T(1,128)S(1)}, u32[]{:S(2)}) copy-start(f32[1,2048]{1,0:T(1,128)S(1)} %add_convert_fusion.2) | copy-start | bytes 24580
  240.9 4.5 copy-start.22
  259.2 4.5 copy-start.22
  273.4 185.4 %reduce-scatter.11.cloned.1.call-start = ((), (), s32[]{:S(2)}) async-start(), calls=%async_computation.12 | async-start | bytes 10485760 | tf_op jit(solution)/shard_map/reduce_scatter | solution.py:75
  314.2 153.1 %copy-start.27 = (f32[1024]{0:T(1024)S(1)}, f32[1024]{0:T(1024)}, u32[]{:S(2)}) copy-start(f32[1024]{0:T(1024)} %param.30) | copy-start | bytes 12292
  314.2 237.6 %all-gather.13.cloned.1.call-start = ((), (), s32[]{:S(2)}) async-start(), calls=%async_computation.13 | async-start | bytes 5242880 | tf_op jit(solution)/shard_map/all_gather | solution.py:61
  470.2 356.8 %reduce-scatter.13.cloned.1.call-start = ((), (), s32[]{:S(2)}) async-start(), calls=%async_computation.14 | async-start | bytes 34603008 | tf_op jit(solution)/shard_map/reduce_scatter | solution.py:69
  571.6 336.4 %all-gather.15.cloned.1.call-start = ((), (), s32[]{:S(2)}) async-start(), calls=%async_computation.15 | async-start | bytes 8650752 | tf_op jit(solution)/shard_map/all_gather | solution.py:65
  833.3 230.0 %reduce-scatter.15.cloned.1.call-start = ((), (), s32[]{:S(2)}) async-start(), calls=%async_computation.16 | async-start | bytes 10485760 | tf_op jit(solution)/shard_map/reduce_scatter | solution.py:75
  918.6 276.0 %all-gather.17.cloned.1.call-start = ((), (), s32[]{:S(2)}) async-start(), calls=%async_computation.17 | async-start | bytes 5242880 | tf_op jit(solution)/shard_map/all_gather | solution.py:61
  1113.8 223.9 %reduce-scatter.17.cloned.1.call-start = ((), (), s32[]{:S(2)}) async-start(), calls=%async_computation.18 | async-start | bytes 17301504 | tf_op jit(solution)/shard_map/reduce_scatter | solution.py:69
  1205.8 283.3 %all-gather.19.cloned.1.call-start = ((), (), s32[]{:S(2)}) async-start(), calls=%async_computation.19 | async-start | bytes 17301504 | tf_op jit(solution)/shard_map/all_gather | solution.py:65
  1348.0 303.8 %reduce-scatter.19.cloned.1.call-start = ((), (), s32[]{:S(2)}) async-start(), calls=%async_computation.20 | async-start | bytes 10485760 | tf_op jit(solution)/shard_map/reduce_scatter | solution.py:75
  1507.2 144.7 %copy-start.5 = (f32[512,1024]{1,0:T(8,128)S(1)}, f32[512,1024]{1,0:T(8,128)}, u32[]{:S(2)}) copy-start(f32[512,1024]{1,0:T(8,128)} %get-tuple-element.355) | copy-start | bytes 6291460
  1507.2 239.5 %all-gather.21.cloned.1.call-start = ((), (), s32[]{:S(2)}) async-start(), calls=%async_computation.21 | async-start | bytes 5242880 | tf_op jit(solution)/shard_map/all_gather | solution.py:61
  1665.0 141.5 %reduce-scatter.21.cloned.1.call-start = ((), (), s32[]{:S(2)}) async-start(), calls=%async_computation.22 | async-start | bytes 6291456 | tf_op jit(solution)/shard_map/reduce_scatter | solution.py:69
  1753.6 199.1 %all-reduce.11.cloned.1.call-start = ((), (), s32[]{:S(2)}) async-start(), calls=%async_computation.24 | async-start | bytes 2097152 | tf_op jit(solution)/shard_map/psum | solution.py:308
  1764.5 44.9 %copy-start.7 = (bf16[2048,1,128]{2,0,1:T(8,128)(2,1)S(1)}, bf16[2048,1,128]{2,0,1:T(8,128)(2,1)}, u32[]{:S(2)}) copy-start(bf16[2048,1,128]{2,0,1:T(8,128)(2,1)} %get-tuple-element.662) | copy-start | bytes 1572868
  1817.1 5.8 copy-start.2
  1867.0 5.8 copy-start.2
  1912.5 19.2 copy-start.12
  1912.6 19.2 copy-start.17
  1912.6 75.3 %all-gather.23.cloned.1.call-start = ((), (), s32[]{:S(2)}) async-start(), calls=%async_computation.23 | async-start | bytes 3145728 | tf_op jit(solution)/shard_map/all_gather | solution.py:65
  1912.6 19.1 copy-start.10
  1934.4 5.9 copy-start.42
  1934.4 261.5 %all-reduce.13.cloned.1.call-start = ((), (), s32[]{:S(2)}) async-start(), calls=%async_computation.26 | async-start | bytes 22544384 | tf_op jit(solution)/shard_map/psum | solution.py:362
  1934.4 5.8 copy-start.41
  1943.6 10.8 copy-start.25
  1943.6 10.8 copy-start.37
  1952.7 4.2 slice-start
  1952.7 4.3 copy-start.40
  1994.1 5.2 copy-start.20
  1994.1 348.8 %reduce-scatter.23.cloned.1.call-start = ((), (), s32[]{:S(2)}) async-start(), calls=%async_computation.25 | async-start | bytes 10485760 | tf_op jit(solution)/shard_map/reduce_scatter | solution.py:75
  2195.9 6.6 copy-start.21
  2199.5 4.6 copy-start.16
  2210.8 132.1 %copy-start.6 = (bf16[512,1024]{1,0:T(8,128)(2,1)S(1)}, bf16[512,1024]{1,0:T(8,128)(2,1)}, u32[]{:S(2)}) copy-start(bf16[512,1024]{1,0:T(8,128)(2,1)} %param.19) | copy-start | bytes 3145732
  2210.8 132.1 %copy-start.26 = (f32[1024]{0:T(1024)S(1)}, f32[1024]{0:T(1024)}, u32[]{:S(2)}) copy-start(f32[1024]{0:T(1024)} %param.25) | copy-start | bytes 12292
  2210.8 132.1 %copy-start.32 = (f32[512]{0:T(512)S(1)}, f32[512]{0:T(512)}, u32[]{:S(2)}) copy-start(f32[512]{0:T(512)} %copy-done.31) | copy-start | bytes 6148
  2214.1 136.1 %copy-start.33 = (f32[1024]{0:T(1024)S(1)}, f32[1024]{0:T(1024)}, u32[]{:S(2)}) copy-start(f32[1024]{0:T(1024)} %get-tuple-element.287) | copy-start | bytes 12292
  2214.1 169.4 %copy-start.35 = (f32[512]{0:T(512)S(1)}, f32[512]{0:T(512)}, u32[]{:S(2)}) copy-start(f32[512]{0:T(512)} %get-tuple-element.380) | copy-start | bytes 6148
  2383.5 4.6 copy-start.1
  (23 other events, 40.7 us)
Sparse Core Ops, SparseCore 0:
  18.6 82.5 all-gather.8
  106.1 61.4 all-reduce.8
  170.6 54.3 reduce-scatter.8
  273.5 33.1 all-gather.10
  314.3 144.4 reduce-scatter.10
  470.3 81.4 all-gather.12
  571.7 255.2 reduce-scatter.12
  833.4 74.4 all-gather.14
  918.8 144.4 reduce-scatter.14
  1113.9 80.7 all-gather.16
  1206.0 131.6 reduce-scatter.16
  1348.1 141.0 all-gather.18
  1507.3 144.4 reduce-scatter.18
  1665.2 81.4 all-gather.20
  1753.7 52.8 reduce-scatter.20
  1912.7 40.0 all-reduce.10
  1954.7 33.1 all-gather.22
  1994.2 201.6 all-reduce.12
  2198.2 144.6 reduce-scatter.22
where the time goes:
time: 2400 us
  waiting for transfers between devices  1880 us (78%)
  matrix products  207 us (9%)
  other arithmetic  128 us (5%)
  blocking collectives  95.1 us (4%)
  local copies, waits for them, and re-layouts  60.3 us (3%)
    reduce_scatter x4, waiting for transfers between devices, partial_rows(): lax.psum_scatter(term(jnp.int32(0), count * lax.axis_size('row')), 'row',...  560 us
    reduce_scatter x4, waiting for transfers between devices, partial_cols(): lax.psum_scatter(term(jnp.int32(0), count * lax.axis_size('col')), 'col',...  477 us
    all_gather x4, waiting for transfers between devices, gather_rows(): return lax.all_gather(values, 'row', axis=0, tiled=True)  319 us
    all_gather x4, waiting for transfers between devices, gather_cols(): return lax.all_gather(values, 'col', axis=0, tiled=True)  277 us
    psum x1, waiting for transfers between devices, body(): lax.psum(grad_query.astype(jnp.bfloat16), 'dp').astype(jnp.float32)  191 us
    psum x1, waiting for transfers between devices, body(): lax.psum(jnp.dot(normed_all, w_kv, preferred_element_type=jnp.float32), '...  49.4 us
  transfers between devices with their start and end apart: 19, of which 19 were waited for; matrix products, arithmetic and copies ran while one was open for 4% of the time, Pallas kernels for 0%

commit v1 on v0

--- a/solution.py
+++ b/solution.py
@@ -124,7 +124,9 @@
         ),
         query_rows,
     )
-    kv_raw = lax.psum(jnp.dot(normed_all, w_kv, preferred_element_type=jnp.float32), "col")
+    kv_raw = jnp.sum(
+        lax.all_gather(jnp.dot(normed_all, w_kv, preferred_element_type=jnp.float32), "col"), axis=0
+    )
     queries = (
         rotary(
             query_raw.reshape(query_rows, key_heads * heads_per_group, HEAD_SIZE), query_pos, 1.0

time: 2400 us -> 2400 us (level)
    psum x1 -> x0, waiting for transfers between devices: 49.4 us -> none  [body(): lax.psum(jnp.dot(normed_all, w_kv, preferred_element_type=jnp.float32), '...]
    all_gather x0 -> x1, waiting for transfers between devices: none -> 43 us  [body(): lax.all_gather(jnp.dot(normed_all, w_kv, preferred_element_type=jnp.float...]
  transfers between devices with their start and end apart: 19 -> 19, of which waited for: 19 -> 19; matrix products, arithmetic and copies ran while one was open for 4% -> 5% of each run, Pallas kernels for 0% -> 0%
where the time goes in v1:
time: 2400 us; the launch traced here: 2390 us
  waiting for transfers between devices  1870 us (78%)
  matrix products  207 us (9%)
  other arithmetic  133 us (6%)
  blocking collectives  95.2 us (4%)
  local copies, waits for them, and re-layouts  60.7 us (3%)
    reduce_scatter x4, waiting for transfers between devices, partial_rows(): lax.psum_scatter(term(jnp.int32(0), count * lax.axis_size('row')), 'row',...  560 us
    reduce_scatter x4, waiting for transfers between devices, partial_cols(): lax.psum_scatter(term(jnp.int32(0), count * lax.axis_size('col')), 'col',...  471 us
    all_gather x4, waiting for transfers between devices, gather_rows(): return lax.all_gather(values, 'row', axis=0, tiled=True)  319 us
    all_gather x4, waiting for transfers between devices, gather_cols(): return lax.all_gather(values, 'col', axis=0, tiled=True)  277 us
    psum x1, waiting for transfers between devices, body(): lax.psum(grad_query.astype(jnp.bfloat16), 'dp').astype(jnp.float32)  191 us
  transfers between devices with their start and end apart: 19, of which 19 were waited for; matrix products, arithmetic and copies ran while one was open for 5% of the time, Pallas kernels for 0%

profile of v1, /device:TPU:0, one launch (start us, length us, event | category | flops | bytes accessed | tf_op | source)
XLA Modules:
  0.0 2390.0 jit_solution(15715515158893792449)
XLA Ops:
  8.9 5.9 psum.112
  20.5 80.6 %all-gather.11.cloned.1.call-done = bf16[2048,1024]{1,0:T(8,128)(2,1)} async-done(((bf16[512,1024]{1,0:T(8,128)(2,1)}), bf16[2048,1024]{1,0:T(8,128)(2,1)}) %all-gather.11.cloned.1.call-update) | async-done | bytes 4194320 | tf_op jit(solution)/shard_map/all_gather | solution.py:61
  106.0 6.9 fusion.91
  118.4 43.0 %all-gather.27.cloned.1.call-done = f32[4096,256]{1,0:T(8,128)} async-done(((f32[2048,256]{1,0:T(8,128)}), f32[4096,256]{1,0:T(8,128)}) %all-gather.27.cloned.1.call-update) | async-done | bytes 4194320 | tf_op jit(solution)/shard_map/all_gather | solution.py:128
  176.3 42.3 %reduce-scatter.9.cloned.1.call-done = f32[1024,512]{1,0:T(8,128)} async-done(((f32[2048,512]{1,0:T(8,128)}), f32[1024,512]{1,0:T(8,128)}) %reduce-scatter.9.cloned.1.call-update) | async-done | bytes 2097168 | tf_op jit(solution)/shard_map/reduce_scatter | solution.py:69
  227.1 36.7 %while.27 = (s32[]{:T(128)}, bf16[2,512,1,4,128]{4,1,3,2,0:T(8,128)(2,1)}, f32[2,1,4,512,1]{3,2,4,1,0:T(4,128)S(1)}, s32[2048]{0:T(1024)S(1)}, s32[2]{0:T(128)S(...) while((s32[]{:T(128)}, ...), condition=%wide.region_9.10_spmd.clone, body=%wide.region_6.9_spmd.clone.sunk | while | flops 2202009600 | bytes 65642824 | solution.py:176
  239.0 5.5 fusion.154
  257.4 5.5 fusion.154
  267.5 32.8 %all-gather.13.cloned.1.call-done = bf16[2048,512]{1,0:T(8,128)(2,1)} async-done(((bf16[1024,512]{1,0:T(8,128)(2,1)}), bf16[2048,512]{1,0:T(8,128)(2,1)}) %all-gather.13.cloned.1.call-update) | async-done | bytes 2097168 | tf_op jit(solution)/shard_map/all_gather | solution.py:65
  300.3 7.5 fusion.93
  308.5 144.0 %reduce-scatter.11.cloned.1.call-done = f32[512,1024]{1,0:T(8,128)} async-done(((f32[2048,1024]{1,0:T(8,128)}), f32[512,1024]{1,0:T(8,128)}) %reduce-scatter.11.cloned.1.call-update) | async-done | bytes 2097168 | tf_op jit(solution)/shard_map/reduce_scatter | solution.py:75
  469.4 76.1 %all-gather.15.cloned.1.call-done = bf16[2048,1024]{1,0:T(8,128)(2,1)} async-done(((bf16[512,1024]{1,0:T(8,128)(2,1)}), bf16[2048,1024]{1,0:T(8,128)(2,1)}) %all-gather.15.cloned.1.call-update) | async-done | bytes 4194320 | tf_op jit(solution)/shard_map/all_gather | solution.py:61
  545.5 19.7 fusion.94
  565.3 255.4 %reduce-scatter.13.cloned.1.call-done = f32[1024,2816]{1,0:T(8,128)} async-done(((f32[2048,2816]{1,0:T(8,128)}), f32[1024,2816]{1,0:T(8,128)}) %reduce-scatter.13.cloned.1.call-update) | async-done | bytes 11534352 | tf_op jit(solution)/shard_map/reduce_scatter | solution.py:69
  820.7 6.3 multiply_convert_fusion.2
  827.0 74.6 %all-gather.17.cloned.1.call-done = bf16[2048,1408]{1,0:T(8,128)(2,1)} async-done(((bf16[1024,1408]{1,0:T(8,128)(2,1)}), bf16[2048,1408]{1,0:T(8,128)(2,1)}) %all-gather.17.cloned.1.call-update) | async-done | bytes 5767184 | tf_op jit(solution)/shard_map/all_gather | solution.py:65
  901.6 10.7 fusion.95
  914.3 142.7 %reduce-scatter.15.cloned.1.call-done = f32[512,1024]{1,0:T(8,128)} async-done(((f32[2048,1024]{1,0:T(8,128)}), f32[512,1024]{1,0:T(8,128)}) %reduce-scatter.15.cloned.1.call-update) | async-done | bytes 2097168 | tf_op jit(solution)/shard_map/reduce_scatter | solution.py:75
  1061.9 41.2 %all-reduce.2 = (f32[]{:T(128)}, f32[]{:T(128)}) all-reduce(f32[]{:T(128)} %get-tuple-element.396, f32[]{:T(128)S(6)} %select_n.47), channel_id=1, replica_groups=mesh['dp'=4,'row'=4,'col'=2] {'dp','row','col'}, use_global_device_ids=true, to_apply=%region_17.18 | all-reduce | flops 2 | bytes 16 | tf_op jit(solution)/shard_map/psum | solution.py:214
  1107.5 80.8 %all-gather.19.cloned.1.call-done = bf16[2048,1024]{1,0:T(8,128)(2,1)} async-done(((bf16[512,1024]{1,0:T(8,128)(2,1)}), bf16[2048,1024]{1,0:T(8,128)(2,1)}) %all-gather.19.cloned.1.call-update) | async-done | bytes 4194320 | tf_op jit(solution)/shard_map/all_gather | solution.py:61
  1188.4 11.2 fusion.96
  1199.6 131.8 %reduce-scatter.17.cloned.1.call-done = f32[1024,1408]{1,0:T(8,128)} async-done(((f32[2048,1408]{1,0:T(8,128)}), f32[1024,1408]{1,0:T(8,128)}) %reduce-scatter.17.cloned.1.call-update) | async-done | bytes 5767184 | tf_op jit(solution)/shard_map/reduce_scatter | solution.py:69
  1331.4 7.4 multiply_convert_fusion.1
  1341.8 141.1 %all-gather.21.cloned.1.call-done = bf16[2048,2816]{1,0:T(8,128)(2,1)} async-done(((bf16[1024,2816]{1,0:T(8,128)(2,1)}), bf16[2048,2816]{1,0:T(8,128)(2,1)}) %all-gather.21.cloned.1.call-update) | async-done | bytes 11534352 | tf_op jit(solution)/shard_map/all_gather | solution.py:65
  1482.9 18.0 fusion.97
  1501.0 144.6 %reduce-scatter.19.cloned.1.call-done = f32[512,1024]{1,0:T(8,128)} async-done(((f32[2048,1024]{1,0:T(8,128)}), f32[512,1024]{1,0:T(8,128)}) %reduce-scatter.19.cloned.1.call-update) | async-done | bytes 2097168 | tf_op jit(solution)/shard_map/reduce_scatter | solution.py:75
  1653.2 5.5 multiply_convert_fusion.3
  1658.8 81.6 %all-gather.23.cloned.1.call-done = bf16[2048,1024]{1,0:T(8,128)(2,1)} async-done(((bf16[512,1024]{1,0:T(8,128)(2,1)}), bf16[2048,1024]{1,0:T(8,128)(2,1)}) %all-gather.23.cloned.1.call-update) | async-done | bytes 4194320 | tf_op jit(solution)/shard_map/all_gather | solution.py:61
  1740.4 6.9 fusion.98
  1747.4 10.9 convolution_convert_fusion.1
  1758.3 42.0 %reduce-scatter.21.cloned.1.call-done = f32[1024,512]{1,0:T(8,128)} async-done(((f32[2048,512]{1,0:T(8,128)}), f32[1024,512]{1,0:T(8,128)}) %reduce-scatter.21.cloned.1.call-update) | async-done | bytes 2097168 | tf_op jit(solution)/shard_map/reduce_scatter | solution.py:69
  1803.1 100.3 %while.28 = (s32[]{:T(128)}, f32[2048,2,128]{0,2,1:T(8,128)}, f32[2,512,1,4,128]{4,1,0,3,2:T(8,128)}, s32[2]{0:T(128)S(1)}, bf16[1024,1,4,128]{3,0,2,1:T(8,128)(...) while((s32[]{:T(128)}, f32[2048,2,128]{0,2,1:T(8,128)}, ...), condition=%wide.region_27.28_spmd.clone.clone, body=%wide.region_25.27_spmd.clone.clone.sunk | while | flops 5437915136 | bytes 244941232 | solution.py:306
  1810.8 5.8 copy-done.2
  1816.6 5.1 fusion.163
  1821.7 12.1 fusion.164
  1833.8 12.1 fusion.165
  1860.7 5.8 copy-done.2
  1866.5 5.1 fusion.163
  1871.6 12.1 fusion.164
  1883.7 12.1 fusion.165
  1906.3 19.1 convolution_convert_fusion
  1928.2 5.8 fusion.88
  1937.3 9.2 all-reduce.8.cloned.1.call-done
  1952.9 28.7 %all-gather.25.cloned.1.call-done = bf16[2048,512]{0,1:T(8,128)(2,1)} async-done(((bf16[1024,512]{0,1:T(8,128)(2,1)}), bf16[2048,512]{0,1:T(8,128)(2,1)}) %all-gather.25.cloned.1.call-update) | async-done | bytes 2097168 | tf_op jit(solution)/shard_map/all_gather | solution.py:65
  1981.7 6.2 convolution_convert_fusion.3
  1998.5 191.2 %all-reduce.10.cloned.1.call-done = (bf16[1024,512]{1,0:T(8,128)(2,1)}, bf16[1024,128]{1,0:T(8,128)(2,1)}, bf16[1024,128]{1,0:T(8,128)(2,1)}, bf16[512,1024]{1,0...) async-done(((bf16[1024,512]{1,0:T(8,128)(2,1)}, bf16[1024,128]{1,0:T(8,128)(2,1)}, bf16[1024,128]{1,0:T(8,128)(2,1)}, ...) | async-done | bytes 11272208 | tf_op jit(solution)/shard_map/psum | solution.py:364
  2207.9 129.0 %reduce-scatter.23.cloned.1.call-done = f32[512,1024]{1,0:T(8,128)} async-done(((f32[2048,1024]{1,0:T(8,128)}), f32[512,1024]{1,0:T(8,128)}) %reduce-scatter.23.cloned.1.call-update) | async-done | bytes 2097168 | tf_op jit(solution)/shard_map/reduce_scatter | solution.py:75
  2344.1 33.4 %all-reduce.3 = (f32[1024]{0:T(1024)}, f32[1024]{0:T(1024)}) all-reduce(f32[1024]{0:T(1024)S(1)} %get-tuple-element.333, f32[1024]{0:T(1024)S(1)} %copy-done.33), channel_id=1, replica_groups=mesh['dp'=4,'row'=4,'col'=2] {'dp','row'}, use_global_device_ids=true, to_apply=%region_33.34 | all-reduce | flops 2048 | bytes 16384 | tf_op jit(solution)/shard_map/psum | solution.py:362
  (253 shorter events, 194.0 us)
Async XLA Ops:
  7.2 894.4 %copy-start = (bf16[1408,1024]{1,0:T(8,128)(2,1)S(1)}, bf16[1408,1024]{1,0:T(8,128)(2,1)}, u32[]{:S(2)}) copy-start(bf16[1408,1024]{1,0:T(8,128)(2,1)} %param.33) | copy-start | bytes 8650756
  7.2 94.0 %all-gather.11.cloned.1.call-start = ((), (), s32[]{:S(2)}) async-start(), calls=%async_computation.8 | async-start | bytes 5242880 | tf_op jit(solution)/shard_map/all_gather | solution.py:61
  18.5 142.9 %all-gather.27.cloned.1.call-start = ((), (), s32[]{:S(2)}) async-start(), calls=%async_computation.25 | async-start | bytes 6291456 | tf_op jit(solution)/shard_map/all_gather | solution.py:128
  20.5 85.4 %copy-start.19 = (bf16[1024,256]{1,0:T(8,128)(2,1)}, bf16[1024,256]{1,0:T(8,128)(2,1)S(1)}, u32[]{:S(2)}) copy-start(bf16[1024,256]{1,0:T(8,128)(2,1)S(1)} %constant_dynamic-update-slice_fusion) | copy-start | bytes 1572868
  106.0 112.6 %reduce-scatter.9.cloned.1.call-start = ((), (), s32[]{:S(2)}) async-start(), calls=%async_computation.9 | async-start | bytes 6291456 | tf_op jit(solution)/shard_map/reduce_scatter | solution.py:69
  112.9 187.4 %all-gather.13.cloned.1.call-start = ((), (), s32[]{:S(2)}) async-start(), calls=%async_computation.10 | async-start | bytes 3145728 | tf_op jit(solution)/shard_map/all_gather | solution.py:65
  113.6 56.6 %copy-start.36 = (f32[64]{0:T(128)}, f32[64]{0:T(128)S(1)}, u32[]{:S(2)}) copy-start(f32[64]{0:T(128)S(1)} %multiply_power_fusion) | copy-start | bytes 772
  115.0 55.2 %copy-start.24 = (f32[1,2048]{1,0:T(1,128)}, f32[1,2048]{1,0:T(1,128)S(1)}, u32[]{:S(2)}) copy-start(f32[1,2048]{1,0:T(1,128)S(1)} %add_convert_fusion.2) | copy-start | bytes 24580
  234.5 4.5 copy-start.22
  252.9 4.5 copy-start.22
  267.0 185.4 %reduce-scatter.11.cloned.1.call-start = ((), (), s32[]{:S(2)}) async-start(), calls=%async_computation.11 | async-start | bytes 10485760 | tf_op jit(solution)/shard_map/reduce_scatter | solution.py:75
  307.8 153.1 %copy-start.27 = (f32[1024]{0:T(1024)S(1)}, f32[1024]{0:T(1024)}, u32[]{:S(2)}) copy-start(f32[1024]{0:T(1024)} %param.30) | copy-start | bytes 12292
  307.8 237.6 %all-gather.15.cloned.1.call-start = ((), (), s32[]{:S(2)}) async-start(), calls=%async_computation.12 | async-start | bytes 5242880 | tf_op jit(solution)/shard_map/all_gather | solution.py:61
  463.8 356.9 %reduce-scatter.13.cloned.1.call-start = ((), (), s32[]{:S(2)}) async-start(), calls=%async_computation.13 | async-start | bytes 34603008 | tf_op jit(solution)/shard_map/reduce_scatter | solution.py:69
  565.2 336.4 %all-gather.17.cloned.1.call-start = ((), (), s32[]{:S(2)}) async-start(), calls=%async_computation.14 | async-start | bytes 8650752 | tf_op jit(solution)/shard_map/all_gather | solution.py:65
  827.0 229.9 %reduce-scatter.15.cloned.1.call-start = ((), (), s32[]{:S(2)}) async-start(), calls=%async_computation.15 | async-start | bytes 10485760 | tf_op jit(solution)/shard_map/reduce_scatter | solution.py:75
  912.3 276.0 %all-gather.19.cloned.1.call-start = ((), (), s32[]{:S(2)}) async-start(), calls=%async_computation.16 | async-start | bytes 5242880 | tf_op jit(solution)/shard_map/all_gather | solution.py:61
  1107.5 223.9 %reduce-scatter.17.cloned.1.call-start = ((), (), s32[]{:S(2)}) async-start(), calls=%async_computation.17 | async-start | bytes 17301504 | tf_op jit(solution)/shard_map/reduce_scatter | solution.py:69
  1199.5 283.3 %all-gather.21.cloned.1.call-start = ((), (), s32[]{:S(2)}) async-start(), calls=%async_computation.18 | async-start | bytes 17301504 | tf_op jit(solution)/shard_map/all_gather | solution.py:65
  1341.7 303.8 %reduce-scatter.19.cloned.1.call-start = ((), (), s32[]{:S(2)}) async-start(), calls=%async_computation.19 | async-start | bytes 10485760 | tf_op jit(solution)/shard_map/reduce_scatter | solution.py:75
  1500.9 144.6 %copy-start.5 = (f32[512,1024]{1,0:T(8,128)S(1)}, f32[512,1024]{1,0:T(8,128)}, u32[]{:S(2)}) copy-start(f32[512,1024]{1,0:T(8,128)} %get-tuple-element.399) | copy-start | bytes 6291460
  1500.9 239.5 %all-gather.23.cloned.1.call-start = ((), (), s32[]{:S(2)}) async-start(), calls=%async_computation.20 | async-start | bytes 5242880 | tf_op jit(solution)/shard_map/all_gather | solution.py:61
  1658.7 141.6 %reduce-scatter.21.cloned.1.call-start = ((), (), s32[]{:S(2)}) async-start(), calls=%async_computation.21 | async-start | bytes 6291456 | tf_op jit(solution)/shard_map/reduce_scatter | solution.py:69
  1747.3 199.1 %all-reduce.8.cloned.1.call-start = ((), (), s32[]{:S(2)}) async-start(), calls=%async_computation.23 | async-start | bytes 2097152 | tf_op jit(solution)/shard_map/psum | solution.py:310
  1758.3 44.9 %copy-start.7 = (bf16[2048,1,128]{2,0,1:T(8,128)(2,1)S(1)}, bf16[2048,1,128]{2,0,1:T(8,128)(2,1)}, u32[]{:S(2)}) copy-start(bf16[2048,1,128]{2,0,1:T(8,128)(2,1)} %get-tuple-element.706) | copy-start | bytes 1572868
  1810.8 5.8 copy-start.2
  1860.7 5.8 copy-start.2
  1906.3 19.2 copy-start.12
  1906.3 19.2 copy-start.17
  1906.3 75.4 %all-gather.25.cloned.1.call-start = ((), (), s32[]{:S(2)}) async-start(), calls=%async_computation.22 | async-start | bytes 3145728 | tf_op jit(solution)/shard_map/all_gather | solution.py:65
  1906.3 19.1 copy-start.10
  1928.1 5.9 copy-start.42
  1928.1 261.6 %all-reduce.10.cloned.1.call-start = ((), (), s32[]{:S(2)}) async-start(), calls=%async_computation.26 | async-start | bytes 22544384 | tf_op jit(solution)/shard_map/psum | solution.py:364
  1928.2 5.8 copy-start.41
  1937.3 10.8 copy-start.25
  1937.3 10.8 copy-start.37
  1946.5 4.2 slice-start
  1946.5 4.3 copy-start.40
  1987.9 5.2 copy-start.20
  1987.9 348.9 %reduce-scatter.23.cloned.1.call-start = ((), (), s32[]{:S(2)}) async-start(), calls=%async_computation.24 | async-start | bytes 10485760 | tf_op jit(solution)/shard_map/reduce_scatter | solution.py:75
  2189.7 6.6 copy-start.21
  2193.3 4.6 copy-start.16
  2204.6 132.2 %copy-start.6 = (bf16[512,1024]{1,0:T(8,128)(2,1)S(1)}, bf16[512,1024]{1,0:T(8,128)(2,1)}, u32[]{:S(2)}) copy-start(bf16[512,1024]{1,0:T(8,128)(2,1)} %param.19) | copy-start | bytes 3145732
  2204.6 132.2 %copy-start.26 = (f32[1024]{0:T(1024)S(1)}, f32[1024]{0:T(1024)}, u32[]{:S(2)}) copy-start(f32[1024]{0:T(1024)} %param.25) | copy-start | bytes 12292
  2204.6 132.2 %copy-start.32 = (f32[512]{0:T(512)S(1)}, f32[512]{0:T(512)}, u32[]{:S(2)}) copy-start(f32[512]{0:T(512)} %copy-done.31) | copy-start | bytes 6148
  2207.9 136.2 %copy-start.33 = (f32[1024]{0:T(1024)S(1)}, f32[1024]{0:T(1024)}, u32[]{:S(2)}) copy-start(f32[1024]{0:T(1024)} %get-tuple-element.331) | copy-start | bytes 12292
  2207.9 169.6 %copy-start.35 = (f32[512]{0:T(512)S(1)}, f32[512]{0:T(512)}, u32[]{:S(2)}) copy-start(f32[512]{0:T(512)} %get-tuple-element.424) | copy-start | bytes 6148
  2377.5 4.6 copy-start.1
  (23 other events, 40.7 us)
Sparse Core Ops, SparseCore 0:
  18.6 82.5 all-gather.10
  106.1 55.2 all-gather.26
  164.3 54.2 reduce-scatter.8
  267.2 33.1 all-gather.12
  307.9 144.4 reduce-scatter.10
  463.9 81.5 all-gather.14
  565.4 255.2 reduce-scatter.12
  827.1 74.4 all-gather.16
  912.4 144.4 reduce-scatter.14
  1107.6 80.7 all-gather.18
  1199.7 131.6 reduce-scatter.16
  1341.8 141.0 all-gather.20
  1501.0 144.4 reduce-scatter.18
  1658.9 81.5 all-gather.22
  1747.4 52.8 reduce-scatter.20
  1906.4 40.0 all-reduce.7
  1948.5 33.1 all-gather.24
  1988.0 201.6 all-reduce.9
  2192.1 144.6 reduce-scatter.22
